TPU v7x, 32 devices: a whole 2x2x4 slice. The times are simulated.
32 devices in a mesh: groups: 2 (over x), row: 16 (over z, y, core).
Axes of the slice: x: 2, y: 2, z: 4, core: 2. Of those that a mesh axis runs over, the one named last changes fastest.
Arguments:
- forces: bfloat16 [2048, 768], P(('groups', 'row')), parts along dimension 0, may hold values from -6 to 6
- tiles: bfloat16 [32768, 96, 96], P(('groups', 'row')), parts along dimension 0, may hold values from -0.109375 to 0.109375
- tile_local: int32 [32768], P(('groups', 'row')), parts along dimension 0, may hold values from 0 to 63
- tile_slot: int32 [32768], P(('groups', 'row')), parts along dimension 0, may hold values from 0 to 255
- tile_flag: int32 [32768], P(('groups', 'row')), parts along dimension 0, may hold values 0 or 1
- want_list: int32 [32, 16, 16], P(('groups', 'row')), parts along dimension 0, may hold values from 0 to 63
Outputs:
- krylov_one: bfloat16 [2048, 768], P(('groups', 'row')), parts along dimension 0
- krylov_two: bfloat16 [2048, 768], P(('groups', 'row')), parts along dimension 0
There are 2 independent parts, one for each index of `groups`. A program takes and returns all parts, laid end to end along the dimension named above; each array names one. Nothing has to cross between parts.
All inputs are finite; a program needn't handle non-finite values. No bound on the sum of `tile_flag` on one device may be relied on, other than what follows from the above.
Results may differ from a plain program's by a relative error of at most 0.0041.
Values may be sent and summed in bfloat16 or wider, within the bound.
No kernel may reach another device: no remote copies, remote signals or barrier semaphores. Data moves between devices by JAX's collectives and lax.ppermute only.
A program may use at most 128 MiB of HBM per device.

v0:
```python
import jax
import jax.numpy as jnp
from jax import lax
from jax.sharding import PartitionSpec as P

NRHS = 8


def one_hot_table(index, count, kind):
    return (index[:, None] == jnp.arange(count, dtype=jnp.int32)[None, :]).astype(kind)


def pick_rows(table, values):
    return jnp.dot(table, values, preferred_element_type=jnp.float32).astype(jnp.bfloat16)


def sum_rows(table, partial_rows):
    return lax.dot_general(
        table,
        partial_rows,
        (((0,), (0,)), ((), ())),
        precision=lax.Precision.HIGHEST,
        preferred_element_type=jnp.float32,
    )


def per_device(forces, tiles, tile_local, tile_slot, tile_flag, want_list):
    peer_count = lax.axis_size("row")
    fibres = forces.shape[0]
    row_width = forces.shape[1]
    unknowns = tiles.shape[1]
    capacity = want_list.shape[2]
    blocks = tiles.shape[0]
    slot_total = peer_count * capacity
    wanted = want_list[0]
    mirror_gate = tile_flag.astype(jnp.float32)[:, None, None]
    local_pick = one_hot_table(tile_local, fibres, jnp.bfloat16)
    local_sum = one_hot_table(tile_local, fibres, jnp.float32)
    slot_pick = one_hot_table(tile_slot, slot_total, jnp.bfloat16)
    slot_sum = one_hot_table(tile_slot, slot_total, jnp.float32)
    global_rows = (jnp.arange(peer_count, dtype=jnp.int32)[:, None] * fibres + wanted).reshape(-1)
    global_pick = one_hot_table(global_rows, fibres * peer_count, jnp.bfloat16)
    global_sum = one_hot_table(global_rows, fibres * peer_count, jnp.float32)

    def operate(current):
        own_forces = pick_rows(local_pick, current).reshape(blocks, NRHS, unknowns)
        mirror = (
            jnp.einsum("kij,kri->krj", tiles, own_forces, preferred_element_type=jnp.float32)
            * mirror_gate
        )
        slot_part = sum_rows(slot_sum, mirror.reshape(blocks, row_width))
        all_rows = lax.all_gather(current, "row", axis=0, tiled=True)
        slot_forces = pick_rows(global_pick, all_rows)
        far_forces = pick_rows(slot_pick, slot_forces).reshape(blocks, NRHS, unknowns)
        direct = jnp.einsum("kij,krj->kri", tiles, far_forces, preferred_element_type=jnp.float32)
        own_part = sum_rows(local_sum, direct.reshape(blocks, row_width))
        dense_part = sum_rows(global_sum, slot_part)
        returned = lax.psum_scatter(dense_part, "row", scatter_dimension=0, tiled=True)
        return (own_part + returned).astype(jnp.bfloat16)

    krylov_one = operate(forces)
    krylov_two = operate(krylov_one)
    return (krylov_one, krylov_two)


def solution(mesh):
    in_specs = (
        P(("groups", "row"), None),
        P(("groups", "row"), None, None),
        P(("groups", "row")),
        P(("groups", "row")),
        P(("groups", "row")),
        P(("groups", "row"), None, None),
    )
    out_specs = (P(("groups", "row"), None), P(("groups", "row"), None))
    return jax.shard_map(
        per_device, mesh=mesh, in_specs=in_specs, out_specs=out_specs, check_vma=False
    )
```

profile of v0, /device:TPU:0, one launch (start us, length us, event | category | flops | bytes accessed | tf_op | source)
XLA Modules:
  0.0 256.3 jit_solution(7490937594834433806)
XLA Ops:
  7.2 0.7 all-gather.3.cloned.1.call-update
  8.0 29.6 %copy.17 = bf16[1024,96,96]{2,1,0:T(8,128)(2,1)} copy(bf16[1024,96,96]{0,2,1:T(8,128)(2,1)} %param.7) | data formatting | bytes 37748736 | tf_op args[1]
  37.6 1.9 convolution_convert_fusion.1
  39.5 3.3 %copy.19 = bf16[1024,8,96]{2,1,0:T(8,128)(2,1)S(1)} copy(bf16[1024,8,96]{0,2,1:T(8,128)(2,1)} %bitcast.30) | data formatting | bytes 3145728 | tf_op jit(solution)/shard_map/reshape | solution.py:46
  42.8 13.6 %broadcast_multiply_fusion.1 = f32[1024,8,96]{2,1,0:T(8,128)} fusion(f32[1024]{0:T(1024)S(1)} %convert_element_type.36, bf16[1024,8,96]{2,1,0:T(8,128)(2,1)S(1)} %copy.19, bf16[1024,96,96]{2,1,0:T(8,128)(2,1)} %copy.17), kind=kOutput, calls=%fused_computation.1 | convolution fusion | flops 151781376 | bytes 23597056 | tf_op jit(solution)/shard_map/kij,kri->krj/dot_general | solution.py:48
  56.4 3.9 %copy.21 = f32[1024,8,96]{0,2,1:T(8,128)S(1)} copy(f32[1024,8,96]{2,1,0:T(8,128)} %broadcast_multiply_fusion.1) | data formatting | bytes 6291456 | tf_op jit(solution)/shard_map/mul | solution.py:48
  60.3 0.1 add.24
  60.4 0.1 add.25
  60.4 0.1 squeeze.3
  60.5 2.0 fusion.7
  62.6 3.4 %fusion.3 = f32[1024,768]{1,0:T(8,128)} fusion(f32[256,768]{1,0:T(8,128)S(1)} %fusion.7, s32[256]{0:T(256)S(1)} %add.26), kind=kOutput, calls=%fused_computation.14 | convolution fusion | flops 2416181248 | bytes 3933184 | tf_op jit(solution)/shard_map/dot_general | solution.py:18
  66.0 0.2 all-gather.5.cloned.1.call-start
  66.2 4.0 %convolution_convert_fusion.3 = bf16[1024,768]{0,1:T(8,128)(2,1)} fusion(bf16[1024,768]{1,0:T(8,128)(2,1)} %all-gather.3.cloned.1.call-done, s32[256]{0:T(256)S(1)} %add.26, s32[1024]{0:T(1024)S(1)} %copy-done.2), kind=kOutput, calls=%fused_computation.5 | convolution fusion | flops 806813696 | bytes 3150848 | tf_op jit(solution)/shard_map/dot_general | solution.py:14
  70.3 3.3 %copy.16 = bf16[1024,8,96]{2,1,0:T(8,128)(2,1)S(1)} copy(bf16[1024,8,96]{0,2,1:T(8,128)(2,1)} %bitcast.33) | data formatting | bytes 3145728 | tf_op jit(solution)/shard_map/reshape | solution.py:54
  73.5 18.1 %fusion.26 = f32[1024,8,96]{2,1,0:T(8,128)} fusion(bf16[1024,8,96]{2,1,0:T(8,128)(2,1)S(1)} %copy.16, bf16[1024,96,96]{2,1,0:T(8,128)(2,1)} %copy.17), kind=kOutput, calls=%fused_computation.34 | convolution fusion | flops 150994944 | bytes 23592960 | tf_op jit(solution)/shard_map/kij,krj->kri/dot_general | solution.py:55
  91.6 3.9 %copy.18 = f32[1024,8,96]{0,2,1:T(8,128)S(1)} copy(f32[1024,8,96]{2,1,0:T(8,128)} %fusion.26) | data formatting | bytes 6291456 | tf_op jit(solution)/shard_map/kij,krj->kri/dot_general | solution.py:55
  95.5 39.6 %reduce-scatter.3.cloned.1.call-done = f32[64,768]{1,0:T(8,128)} async-done(((f32[1024,768]{1,0:T(8,128)}), f32[64,768]{1,0:T(8,128)}) %reduce-scatter.3.cloned.1.call-update) | async-done | bytes 196624 | tf_op jit(solution)/shard_map/reduce_scatter | solution.py:58
  135.1 3.5 %fusion = bf16[64,768]{1,0:T(8,128)(2,1)} fusion(f32[64,768]{1,0:T(8,128)} %reduce-scatter.3.cloned.1.call-done, f32[1024,768]{0,1:T(8,128)S(1)} %bitcast.28, s32[1024]{0:T(1024)S(1)} %copy-done.1), kind=kOutput, calls=%fused_computation.10 | convolution fusion | flops 604209152 | bytes 3444736 | tf_op jit(solution)/shard_map/dot_general | solution.py:18
  138.7 0.3 reduce-scatter.5.cloned.1.call-start
  138.9 2.8 %convolution_convert_fusion = bf16[1024,768]{0,1:T(8,128)(2,1)} fusion(bf16[64,768]{1,0:T(8,128)(2,1)} %fusion, s32[1024]{0:T(1024)S(1)} %copy-done.1), kind=kOutput, calls=%fused_computation.2 | convolution fusion | flops 101515264 | bytes 1675264 | tf_op jit(solution)/shard_map/dot_general | solution.py:14
  141.7 3.3 %copy.25 = bf16[1024,8,96]{2,1,0:T(8,128)(2,1)S(1)} copy(bf16[1024,8,96]{0,2,1:T(8,128)(2,1)} %bitcast.31) | data formatting | bytes 3145728 | tf_op jit(solution)/shard_map/reshape | solution.py:46
  145.0 13.6 %broadcast_multiply_fusion = f32[1024,8,96]{2,1,0:T(8,128)} fusion(f32[1024]{0:T(1024)S(1)} %convert_element_type.36, bf16[1024,8,96]{2,1,0:T(8,128)(2,1)S(1)} %copy.25, bf16[1024,96,96]{2,1,0:T(8,128)(2,1)} %copy.17), kind=kOutput, calls=%fused_computation | convolution fusion | flops 151781376 | bytes 23597056 | tf_op jit(solution)/shard_map/kij,kri->krj/dot_general | solution.py:48
  158.5 3.9 %copy.27 = f32[1024,8,96]{0,2,1:T(8,128)S(1)} copy(f32[1024,8,96]{2,1,0:T(8,128)} %broadcast_multiply_fusion) | data formatting | bytes 6291456 | tf_op jit(solution)/shard_map/mul | solution.py:48
  162.4 2.0 fusion.5
  164.4 3.4 %fusion.2 = f32[1024,768]{1,0:T(8,128)} fusion(f32[256,768]{1,0:T(8,128)S(1)} %fusion.5, s32[256]{0:T(256)S(1)} %add.26), kind=kOutput, calls=%fused_computation.13 | convolution fusion | flops 2416181248 | bytes 3933184 | tf_op jit(solution)/shard_map/dot_general | solution.py:18
  167.8 9.6 %all-gather.5.cloned.1.call-done = bf16[1024,768]{1,0:T(8,128)(2,1)} async-done(((bf16[64,768]{1,0:T(8,128)(2,1)}), bf16[1024,768]{1,0:T(8,128)(2,1)}) %all-gather.5.cloned.1.call-update) | async-done | bytes 1572880 | tf_op jit(solution)/shard_map/all_gather | solution.py:52
  177.5 4.0 %convolution_convert_fusion.2 = bf16[1024,768]{0,1:T(8,128)(2,1)} fusion(bf16[1024,768]{1,0:T(8,128)(2,1)} %all-gather.5.cloned.1.call-done, s32[256]{0:T(256)S(1)} %add.26, s32[1024]{0:T(1024)S(1)} %copy-done.2), kind=kOutput, calls=%fused_computation.4 | convolution fusion | flops 806813696 | bytes 3150848 | tf_op jit(solution)/shard_map/dot_general | solution.py:14
  181.5 3.3 %copy.22 = bf16[1024,8,96]{2,1,0:T(8,128)(2,1)S(1)} copy(bf16[1024,8,96]{0,2,1:T(8,128)(2,1)} %bitcast.32) | data formatting | bytes 3145728 | tf_op jit(solution)/shard_map/reshape | solution.py:54
  184.8 18.1 %fusion.27 = f32[1024,8,96]{2,1,0:T(8,128)} fusion(bf16[1024,8,96]{2,1,0:T(8,128)(2,1)S(1)} %copy.22, bf16[1024,96,96]{2,1,0:T(8,128)(2,1)} %copy.17), kind=kOutput, calls=%fused_computation.35 | convolution fusion | flops 150994944 | bytes 23592960 | tf_op jit(solution)/shard_map/kij,krj->kri/dot_general | solution.py:55
  202.9 3.9 %copy.24 = f32[1024,8,96]{0,2,1:T(8,128)S(1)} copy(f32[1024,8,96]{2,1,0:T(8,128)} %fusion.27) | data formatting | bytes 6291456 | tf_op jit(solution)/shard_map/kij,krj->kri/dot_general | solution.py:55
  206.7 39.6 %reduce-scatter.5.cloned.1.call-done = f32[64,768]{1,0:T(8,128)} async-done(((f32[1024,768]{1,0:T(8,128)}), f32[64,768]{1,0:T(8,128)}) %reduce-scatter.5.cloned.1.call-update) | async-done | bytes 196624 | tf_op jit(solution)/shard_map/reduce_scatter | solution.py:58
  246.3 3.5 %fusion.1 = bf16[64,768]{1,0:T(8,128)(2,1)} fusion(f32[64,768]{1,0:T(8,128)} %reduce-scatter.5.cloned.1.call-done, f32[1024,768]{0,1:T(8,128)S(1)} %bitcast.29, s32[1024]{0:T(1024)S(1)} %copy-done.1), kind=kOutput, calls=%fused_computation.11 | convolution fusion | flops 604209152 | bytes 3444736 | tf_op jit(solution)/shard_map/dot_general | solution.py:18
  (19 shorter events, 0.2 us)
Async XLA Ops:
  7.2 59.0 %all-gather.3.cloned.1.call-start = ((), (), s32[]{:S(2)}) async-start(), calls=%async_computation.2 | async-start | bytes 1671168 | tf_op jit(solution)/shard_map/all_gather | solution.py:52
  7.9 29.7 %copy-start.4 = (s32[1024]{0:T(1024)S(1)}, s32[1024]{0:T(1024)}, u32[]{:S(2)}) copy-start(s32[1024]{0:T(1024)} %param.10) | copy-start | bytes 12292
  7.9 29.7 %copy-start = (bf16[64,768]{1,0:T(8,128)(2,1)S(1)}, bf16[64,768]{1,0:T(8,128)(2,1)}, u32[]{:S(2)}) copy-start(bf16[64,768]{1,0:T(8,128)(2,1)} %param.6) | copy-start | bytes 294916
  7.9 29.7 %copy-start.1 = (s32[1024]{0:T(1024)S(1)}, s32[1024]{0:T(1024)}, u32[]{:S(2)}) copy-start(s32[1024]{0:T(1024)} %param.8) | copy-start | bytes 12292
  7.9 127.2 %reduce-scatter.3.cloned.1.call-start = ((), (), s32[]{:S(2)}) async-start(), calls=%async_computation.3 | async-start | bytes 3342336 | tf_op jit(solution)/shard_map/reduce_scatter | solution.py:58
  56.4 4.1 %copy-start.3 = (s32[1,16,16]{2,1,0:T(8,128)S(1)}, s32[1,16,16]{2,1,0:T(8,128)}, u32[]{:S(2)}) copy-start(s32[1,16,16]{2,1,0:T(8,128)} %param.11) | copy-start | bytes 3076
  56.4 4.1 %copy-start.2 = (s32[1024]{0:T(1024)S(1)}, s32[1024]{0:T(1024)}, u32[]{:S(2)}) copy-start(s32[1024]{0:T(1024)} %param.9) | copy-start | bytes 12292
  66.0 111.5 %all-gather.5.cloned.1.call-start = ((), (), s32[]{:S(2)}) async-start(), calls=%async_computation.4 | async-start | bytes 1671168 | tf_op jit(solution)/shard_map/all_gather | solution.py:52
  138.7 107.6 %reduce-scatter.5.cloned.1.call-start = ((), (), s32[]{:S(2)}) async-start(), calls=%async_computation.5 | async-start | bytes 3342336 | tf_op jit(solution)/shard_map/reduce_scatter | solution.py:58
Sparse Core Ops, SparseCore 0:
  10.3 42.3 all-gather.2
  66.1 69.0 reduce-scatter.2
  138.8 38.6 all-gather.4
  181.1 65.1 reduce-scatter.4
where the time goes:
time: 258 us; the launch traced here: 256 us
  matrix products  93.9 us (36%)
  waiting for transfers between devices  89.6 us (35%)
  local copies, waits for them, and re-layouts  58.4 us (23%)
  between operations  13.9 us (5%)
    reduce_scatter x2, waiting for transfers between devices, operate(): lax.psum_scatter(dense_part, 'row', scatter_dimension=0, tiled=True)  79.2 us
    dot_general x2, matrix products, operate(): jnp.einsum('kij,krj->kri', tiles, far_forces, preferred_element_type=jnp....  36.2 us
    unnamed x11, local copies, waits for them, and re-layouts  29.6 us
    dot_general x2, matrix products, operate(): jnp.einsum('kij,kri->krj', tiles, own_forces, preferred_element_type=jnp....  27.1 us
    dot_general x6, matrix products, sum_rows(): lax.dot_general(table, partial_rows, (((0,), (0,)), ((), ())), precision=...  17.8 us
    dot_general x4, matrix products, pick_rows(): jnp.dot(table, values, preferred_element_type=jnp.float32)  12.8 us
    all_gather x2, waiting for transfers between devices, operate(): all_rows = lax.all_gather(current, 'row', axis=0, tiled=True)  9.66 us
    mul x2, local copies, waits for them, and re-layouts, operate(): jnp.einsum('kij,kri->krj', tiles, own_forces, preferred_element_type=jnp....  7.74 us
  transfers between devices with their start and end apart: 4, of which 3 were waited for; matrix products, arithmetic and copies ran while one was open for 57% of the time, Pallas kernels for 0%

commit v1 on v0

--- a/solution.py
+++ b/solution.py
@@ -49,7 +49,14 @@
             * mirror_gate
         )
         slot_part = sum_rows(slot_sum, mirror.reshape(blocks, row_width))
-        all_rows = lax.all_gather(current, "row", axis=0, tiled=True)
+        ring = [current]
+        for hop in range(15):
+            ring.append(lax.ppermute(ring[-1], "row", [(dev, (dev + 1) % 16) for dev in range(16)]))
+        all_rows = jnp.roll(
+            jnp.concatenate(ring[::-1], axis=0),
+            (lax.axis_index("row") + 1) * ring[0].shape[0],
+            axis=0,
+        )
         slot_forces = pick_rows(global_pick, all_rows)
         far_forces = pick_rows(slot_pick, slot_forces).reshape(blocks, NRHS, unknowns)
         direct = jnp.einsum("kij,krj->kri", tiles, far_forces, preferred_element_type=jnp.float32)

time: 258 us -> 356 us (1.38)
  waiting for transfers between devices: 89.6 us -> 177 us
  local copies, waits for them, and re-layouts: 58.4 us -> 67.4 us
    ppermute x0 -> x30, waiting for transfers between devices: none -> 165 us  [operate(): lax.ppermute(ring[-1], 'row', [(dev, (dev + 1) % 16) for dev in range(16)])]
    reduce_scatter x2, waiting for transfers between devices: 79.2 us -> 12.7 us  [operate(): lax.psum_scatter(dense_part, 'row', scatter_dimension=0, tiled=True)]
    all_gather x2 -> x0, waiting for transfers between devices: 9.66 us -> none  [operate(): all_rows = lax.all_gather(current, 'row', axis=0, tiled=True)]
    unnamed x11 -> x65, local copies, waits for them, and re-layouts: 29.6 us -> 37.8 us
  transfers between devices with their start and end apart: 4 -> 32, of which waited for: 3 -> 29; matrix products, arithmetic and copies ran while one was open for 57% -> 43% of each run, Pallas kernels for 0% -> 0%
where the time goes in v1:
time: 356 us; the launch traced here: 354 us
  waiting for transfers between devices  177 us (50%)
  matrix products  93.6 us (26%)
  local copies, waits for them, and re-layouts  67.4 us (19%)
  between operations  14.5 us (4%)
    ppermute x30, waiting for transfers between devices, operate(): lax.ppermute(ring[-1], 'row', [(dev, (dev + 1) % 16) for dev in range(16)])  165 us
    unnamed x65, local copies, waits for them, and re-layouts  37.8 us
    dot_general x2, matrix products, operate(): jnp.einsum('kij,krj->kri', tiles, far_forces, preferred_element_type=jnp....  35.9 us
    dot_general x2, matrix products, operate(): jnp.einsum('kij,kri->krj', tiles, own_forces, preferred_element_type=jnp....  27.1 us
    dot_general x6, matrix products, sum_rows(): lax.dot_general(table, partial_rows, (((0,), (0,)), ((), ())), precision=...  19.1 us
    reduce_scatter x2, waiting for transfers between devices, operate(): lax.psum_scatter(dense_part, 'row', scatter_dimension=0, tiled=True)  12.7 us
    dot_general x4, matrix products, pick_rows(): jnp.dot(table, values, preferred_element_type=jnp.float32)  11.5 us
    dot_general x2, local copies, waits for them, and re-layouts, operate(): jnp.einsum('kij,krj->kri', tiles, far_forces, preferred_element_type=jnp....  7.75 us
  transfers between devices with their start and end apart: 32, of which 29 were waited for; matrix products, arithmetic and copies ran while one was open for 43% of the time, Pallas kernels for 0%

profile of v1, /device:TPU:0, one launch (start us, length us, event | category | flops | bytes accessed | tf_op | source)
XLA Modules:
  0.0 354.1 jit_solution(13769869505717012495)
XLA Ops:
  7.7 7.5 %collective-permute-done = bf16[64,768]{1,0:T(8,128)(2,1)S(1)} collective-permute-done((bf16[64,768]{1,0:T(8,128)(2,1)}, bf16[64,768]{1,0:T(8,128)(2,1)S(1)}, u32[]{:S(2)}, u32[]{:S(2)}) %collective-permute-start) | collective-permute-done | bytes 98336 | tf_op jit(solution)/shard_map/ppermute | solution.py:54
  15.2 6.7 %collective-permute-done.1 = bf16[64,768]{1,0:T(8,128)(2,1)S(1)} collective-permute-done((bf16[64,768]{1,0:T(8,128)(2,1)S(1)}, bf16[64,768]{1,0:T(8,128)(2,1)S(1)}, u32[]{:S(2)}, u32[]{:S(2)}) %collective-permute-start.1) | collective-permute-done | bytes 98336 | tf_op jit(solution)/shard_map/ppermute | solution.py:54
  22.0 6.7 %collective-permute-done.2 = bf16[64,768]{1,0:T(8,128)(2,1)S(1)} collective-permute-done((bf16[64,768]{1,0:T(8,128)(2,1)S(1)}, bf16[64,768]{1,0:T(8,128)(2,1)S(1)}, u32[]{:S(2)}, u32[]{:S(2)}) %collective-permute-start.2) | collective-permute-done | bytes 98336 | tf_op jit(solution)/shard_map/ppermute | solution.py:54
  28.7 6.7 %collective-permute-done.3 = bf16[64,768]{1,0:T(8,128)(2,1)S(1)} collective-permute-done((bf16[64,768]{1,0:T(8,128)(2,1)S(1)}, bf16[64,768]{1,0:T(8,128)(2,1)S(1)}, u32[]{:S(2)}, u32[]{:S(2)}) %collective-permute-start.3) | collective-permute-done | bytes 98336 | tf_op jit(solution)/shard_map/ppermute | solution.py:54
  35.5 6.7 %collective-permute-done.4 = bf16[64,768]{1,0:T(8,128)(2,1)S(1)} collective-permute-done((bf16[64,768]{1,0:T(8,128)(2,1)S(1)}, bf16[64,768]{1,0:T(8,128)(2,1)S(1)}, u32[]{:S(2)}, u32[]{:S(2)}) %collective-permute-start.4) | collective-permute-done | bytes 98336 | tf_op jit(solution)/shard_map/ppermute | solution.py:54
  42.8 6.7 %collective-permute-done.5 = bf16[64,768]{1,0:T(8,128)(2,1)S(1)} collective-permute-done((bf16[64,768]{1,0:T(8,128)(2,1)S(1)}, bf16[64,768]{1,0:T(8,128)(2,1)S(1)}, u32[]{:S(2)}, u32[]{:S(2)}) %collective-permute-start.5) | collective-permute-done | bytes 98336 | tf_op jit(solution)/shard_map/ppermute | solution.py:54
  55.7 29.6 %copy.17 = bf16[1024,96,96]{2,1,0:T(8,128)(2,1)} copy(bf16[1024,96,96]{0,2,1:T(8,128)(2,1)} %param.9) | data formatting | bytes 37748736 | tf_op args[1]
  85.3 13.5 %broadcast_multiply_fusion.1 = f32[1024,8,96]{2,1,0:T(8,128)} fusion(f32[1024]{0:T(1024)S(1)} %convert_element_type.36, bf16[1024,8,96]{2,1,0:T(8,128)(2,1)S(1)} %copy.19, bf16[1024,96,96]{2,1,0:T(8,128)(2,1)} %copy.17), kind=kOutput, calls=%fused_computation.5 | convolution fusion | flops 151781376 | bytes 23597056 | tf_op jit(solution)/shard_map/kij,kri->krj/dot_general | solution.py:48
  105.7 4.1 %collective-permute-done.8 = bf16[64,768]{1,0:T(8,128)(2,1)} collective-permute-done((bf16[64,768]{1,0:T(8,128)(2,1)}, bf16[64,768]{1,0:T(8,128)(2,1)}, u32[]{:S(2)}, u32[]{:S(2)}) %collective-permute-start.8) | collective-permute-done | bytes 98336 | tf_op jit(solution)/shard_map/ppermute | solution.py:54
  110.8 6.0 %collective-permute-done.9 = bf16[64,768]{1,0:T(8,128)(2,1)S(1)} collective-permute-done((bf16[64,768]{1,0:T(8,128)(2,1)}, bf16[64,768]{1,0:T(8,128)(2,1)S(1)}, u32[]{:S(2)}, u32[]{:S(2)}) %collective-permute-start.9) | collective-permute-done | bytes 98336 | tf_op jit(solution)/shard_map/ppermute | solution.py:54
  116.8 4.5 %fusion.19 = f32[1024,768]{1,0:T(8,128)} fusion(f32[256,768]{1,0:T(8,128)} %fusion.23, s32[256]{0:T(256)S(1)} %add.38), kind=kOutput, calls=%fused_computation.22 | convolution fusion | flops 2416181248 | bytes 3933184 | tf_op jit(solution)/shard_map/dot_general | solution.py:18
  123.5 6.7 %collective-permute-done.11 = bf16[64,768]{1,0:T(8,128)(2,1)S(1)} collective-permute-done((bf16[64,768]{1,0:T(8,128)(2,1)S(1)}, bf16[64,768]{1,0:T(8,128)(2,1)S(1)}, u32[]{:S(2)}, u32[]{:S(2)}) %collective-permute-start.11) | collective-permute-done | bytes 98336 | tf_op jit(solution)/shard_map/ppermute | solution.py:54
  130.3 6.7 %collective-permute-done.12 = bf16[64,768]{1,0:T(8,128)(2,1)S(1)} collective-permute-done((bf16[64,768]{1,0:T(8,128)(2,1)S(1)}, bf16[64,768]{1,0:T(8,128)(2,1)S(1)}, u32[]{:S(2)}, u32[]{:S(2)}) %collective-permute-start.12) | collective-permute-done | bytes 98336 | tf_op jit(solution)/shard_map/ppermute | solution.py:54
  137.0 6.7 %collective-permute-done.13 = bf16[64,768]{1,0:T(8,128)(2,1)S(1)} collective-permute-done((bf16[64,768]{1,0:T(8,128)(2,1)S(1)}, bf16[64,768]{1,0:T(8,128)(2,1)S(1)}, u32[]{:S(2)}, u32[]{:S(2)}) %collective-permute-start.13) | collective-permute-done | bytes 98336 | tf_op jit(solution)/shard_map/ppermute | solution.py:54
  143.8 6.7 %collective-permute-done.14 = bf16[64,768]{1,0:T(8,128)(2,1)S(1)} collective-permute-done((bf16[64,768]{1,0:T(8,128)(2,1)S(1)}, bf16[64,768]{1,0:T(8,128)(2,1)S(1)}, u32[]{:S(2)}, u32[]{:S(2)}) %collective-permute-start.14) | collective-permute-done | bytes 98336 | tf_op jit(solution)/shard_map/ppermute | solution.py:54
  160.2 17.9 %fusion.50 = f32[1024,8,96]{2,1,0:T(8,128)} fusion(bf16[1024,8,96]{2,1,0:T(8,128)(2,1)S(1)} %copy.16, bf16[1024,96,96]{2,1,0:T(8,128)(2,1)} %copy.17), kind=kOutput, calls=%fused_computation.78 | convolution fusion | flops 150994944 | bytes 23592960 | tf_op jit(solution)/shard_map/kij,krj->kri/dot_general | solution.py:62
  182.0 7.3 %reduce-scatter.3.cloned.1.call-done = f32[64,768]{1,0:T(8,128)} async-done(((f32[1024,768]{1,0:T(8,128)}), f32[64,768]{1,0:T(8,128)}) %reduce-scatter.3.cloned.1.call-update) | async-done | bytes 196624 | tf_op jit(solution)/shard_map/reduce_scatter | solution.py:65
  192.2 6.7 %collective-permute-done.15 = bf16[64,768]{1,0:T(8,128)(2,1)S(1)} collective-permute-done((bf16[64,768]{1,0:T(8,128)(2,1)S(1)}, bf16[64,768]{1,0:T(8,128)(2,1)S(1)}, u32[]{:S(2)}, u32[]{:S(2)}) %collective-permute-start.15) | collective-permute-done | bytes 98336 | tf_op jit(solution)/shard_map/ppermute | solution.py:54
  198.9 6.7 %collective-permute-done.16 = bf16[64,768]{1,0:T(8,128)(2,1)S(1)} collective-permute-done((bf16[64,768]{1,0:T(8,128)(2,1)S(1)}, bf16[64,768]{1,0:T(8,128)(2,1)S(1)}, u32[]{:S(2)}, u32[]{:S(2)}) %collective-permute-start.16) | collective-permute-done | bytes 98336 | tf_op jit(solution)/shard_map/ppermute | solution.py:54
  205.7 6.7 %collective-permute-done.17 = bf16[64,768]{1,0:T(8,128)(2,1)S(1)} collective-permute-done((bf16[64,768]{1,0:T(8,128)(2,1)S(1)}, bf16[64,768]{1,0:T(8,128)(2,1)S(1)}, u32[]{:S(2)}, u32[]{:S(2)}) %collective-permute-start.17) | collective-permute-done | bytes 98336 | tf_op jit(solution)/shard_map/ppermute | solution.py:54
  212.4 6.7 %collective-permute-done.18 = bf16[64,768]{1,0:T(8,128)(2,1)S(1)} collective-permute-done((bf16[64,768]{1,0:T(8,128)(2,1)S(1)}, bf16[64,768]{1,0:T(8,128)(2,1)S(1)}, u32[]{:S(2)}, u32[]{:S(2)}) %collective-permute-start.18) | collective-permute-done | bytes 98336 | tf_op jit(solution)/shard_map/ppermute | solution.py:54
  219.8 6.7 %collective-permute-done.19 = bf16[64,768]{1,0:T(8,128)(2,1)S(1)} collective-permute-done((bf16[64,768]{1,0:T(8,128)(2,1)S(1)}, bf16[64,768]{1,0:T(8,128)(2,1)S(1)}, u32[]{:S(2)}, u32[]{:S(2)}) %collective-permute-start.19) | collective-permute-done | bytes 98336 | tf_op jit(solution)/shard_map/ppermute | solution.py:54
  227.2 6.7 %collective-permute-done.20 = bf16[64,768]{1,0:T(8,128)(2,1)S(1)} collective-permute-done((bf16[64,768]{1,0:T(8,128)(2,1)S(1)}, bf16[64,768]{1,0:T(8,128)(2,1)S(1)}, u32[]{:S(2)}, u32[]{:S(2)}) %collective-permute-start.20) | collective-permute-done | bytes 98336 | tf_op jit(solution)/shard_map/ppermute | solution.py:54
  234.5 6.7 %collective-permute-done.21 = bf16[64,768]{1,0:T(8,128)(2,1)S(1)} collective-permute-done((bf16[64,768]{1,0:T(8,128)(2,1)S(1)}, bf16[64,768]{1,0:T(8,128)(2,1)S(1)}, u32[]{:S(2)}, u32[]{:S(2)}) %collective-permute-start.21) | collective-permute-done | bytes 98336 | tf_op jit(solution)/shard_map/ppermute | solution.py:54
  248.1 13.5 %broadcast_multiply_fusion = f32[1024,8,96]{2,1,0:T(8,128)} fusion(f32[1024]{0:T(1024)S(1)} %convert_element_type.36, bf16[1024,8,96]{2,1,0:T(8,128)(2,1)S(1)} %copy.25, bf16[1024,96,96]{2,1,0:T(8,128)(2,1)} %copy.17), kind=kOutput, calls=%fused_computation.4 | convolution fusion | flops 151781376 | bytes 23597056 | tf_op jit(solution)/shard_map/kij,kri->krj/dot_general | solution.py:48
  267.8 5.0 %collective-permute-done.24 = bf16[64,768]{1,0:T(8,128)(2,1)} collective-permute-done((bf16[64,768]{1,0:T(8,128)(2,1)}, bf16[64,768]{1,0:T(8,128)(2,1)}, u32[]{:S(2)}, u32[]{:S(2)}) %collective-permute-start.24) | collective-permute-done | bytes 98336 | tf_op jit(solution)/shard_map/ppermute | solution.py:54
  279.8 6.7 %collective-permute-done.26 = bf16[64,768]{1,0:T(8,128)(2,1)S(1)} collective-permute-done((bf16[64,768]{1,0:T(8,128)(2,1)S(1)}, bf16[64,768]{1,0:T(8,128)(2,1)S(1)}, u32[]{:S(2)}, u32[]{:S(2)}) %collective-permute-start.26) | collective-permute-done | bytes 98336 | tf_op jit(solution)/shard_map/ppermute | solution.py:54
  286.5 6.7 %collective-permute-done.27 = bf16[64,768]{1,0:T(8,128)(2,1)S(1)} collective-permute-done((bf16[64,768]{1,0:T(8,128)(2,1)S(1)}, bf16[64,768]{1,0:T(8,128)(2,1)S(1)}, u32[]{:S(2)}, u32[]{:S(2)}) %collective-permute-start.27) | collective-permute-done | bytes 98336 | tf_op jit(solution)/shard_map/ppermute | solution.py:54
  293.3 6.7 %collective-permute-done.28 = bf16[64,768]{1,0:T(8,128)(2,1)S(1)} collective-permute-done((bf16[64,768]{1,0:T(8,128)(2,1)S(1)}, bf16[64,768]{1,0:T(8,128)(2,1)S(1)}, u32[]{:S(2)}, u32[]{:S(2)}) %collective-permute-start.28) | collective-permute-done | bytes 98336 | tf_op jit(solution)/shard_map/ppermute | solution.py:54
  300.0 6.7 %collective-permute-done.29 = bf16[64,768]{1,0:T(8,128)(2,1)S(1)} collective-permute-done((bf16[64,768]{1,0:T(8,128)(2,1)S(1)}, bf16[64,768]{1,0:T(8,128)(2,1)S(1)}, u32[]{:S(2)}, u32[]{:S(2)}) %collective-permute-start.29) | collective-permute-done | bytes 98336 | tf_op jit(solution)/shard_map/ppermute | solution.py:54
  316.4 18.0 %fusion.51 = f32[1024,8,96]{2,1,0:T(8,128)} fusion(bf16[1024,8,96]{2,1,0:T(8,128)(2,1)S(1)} %copy.22, bf16[1024,96,96]{2,1,0:T(8,128)(2,1)} %copy.17), kind=kOutput, calls=%fused_computation.79 | convolution fusion | flops 150994944 | bytes 23592960 | tf_op jit(solution)/shard_map/kij,krj->kri/dot_general | solution.py:62
  338.3 5.4 %reduce-scatter.5.cloned.1.call-done = f32[64,768]{1,0:T(8,128)} async-done(((f32[1024,768]{1,0:T(8,128)}), f32[64,768]{1,0:T(8,128)}) %reduce-scatter.5.cloned.1.call-update) | async-done | bytes 196624 | tf_op jit(solution)/shard_map/reduce_scatter | solution.py:65
  (129 shorter events, 72.4 us)
Async XLA Ops:
  7.2 182.1 %reduce-scatter.3.cloned.1.call-start = ((), (), s32[]{:S(2)}) async-start(), calls=%async_computation.2 | async-start | bytes 3342336 | tf_op jit(solution)/shard_map/reduce_scatter | solution.py:65
  7.2 8.0 %collective-permute-start = (bf16[64,768]{1,0:T(8,128)(2,1)}, bf16[64,768]{1,0:T(8,128)(2,1)S(1)}, u32[]{:S(2)}, u32[]{:S(2)}) collective-permute-start(bf16[64,768]{1,0:T(8,128)(2,1)} %param.8), channel_id=1, source_target_pairs={{0,1},{1,2},{2,3},{3,4},{4,5},{5,6},{6,7},{7,8},{8,9},{9,10},{10,1... | collective-permute-start | bytes 294920 | tf_op jit(solution)/shard_map/ppermute | solution.py:54
  15.2 6.7 %collective-permute-start.1 = (bf16[64,768]{1,0:T(8,128)(2,1)S(1)}, bf16[64,768]{1,0:T(8,128)(2,1)S(1)}, u32[]{:S(2)}, u32[]{:S(2)}) collective-permute-start(bf16[64,768]{1,0:T(8,128)(2,1)S(1)} %collective-permute-done), channel_id=1, source_target_pairs={{0,1},{1,2},{2,3},{3,4},{4,5},{5,6},{6,7},{7,8},{8,9},{9,10},{10,1... | collective-permute-start | bytes 294920 | tf_op jit(solution)/shard_map/ppermute | solution.py:54
  22.0 6.7 %collective-permute-start.2 = (bf16[64,768]{1,0:T(8,128)(2,1)S(1)}, bf16[64,768]{1,0:T(8,128)(2,1)S(1)}, u32[]{:S(2)}, u32[]{:S(2)}) collective-permute-start(bf16[64,768]{1,0:T(8,128)(2,1)S(1)} %collective-permute-done.1), channel_id=1, source_target_pairs={{0,1},{1,2},{2,3},{3,4},{4,5},{5,6},{6,7},{7,8},{8,9},{9,10},{10,1... | collective-permute-start | bytes 294920 | tf_op jit(solution)/shard_map/ppermute | solution.py:54
  28.7 6.7 %collective-permute-start.3 = (bf16[64,768]{1,0:T(8,128)(2,1)S(1)}, bf16[64,768]{1,0:T(8,128)(2,1)S(1)}, u32[]{:S(2)}, u32[]{:S(2)}) collective-permute-start(bf16[64,768]{1,0:T(8,128)(2,1)S(1)} %collective-permute-done.2), channel_id=1, source_target_pairs={{0,1},{1,2},{2,3},{3,4},{4,5},{5,6},{6,7},{7,8},{8,9},{9,10},{10,1... | collective-permute-start | bytes 294920 | tf_op jit(solution)/shard_map/ppermute | solution.py:54
  35.4 6.7 %collective-permute-start.4 = (bf16[64,768]{1,0:T(8,128)(2,1)S(1)}, bf16[64,768]{1,0:T(8,128)(2,1)S(1)}, u32[]{:S(2)}, u32[]{:S(2)}) collective-permute-start(bf16[64,768]{1,0:T(8,128)(2,1)S(1)} %collective-permute-done.3), channel_id=1, source_target_pairs={{0,1},{1,2},{2,3},{3,4},{4,5},{5,6},{6,7},{7,8},{8,9},{9,10},{10,1... | collective-permute-start | bytes 294920 | tf_op jit(solution)/shard_map/ppermute | solution.py:54
  42.8 6.7 %collective-permute-start.5 = (bf16[64,768]{1,0:T(8,128)(2,1)S(1)}, bf16[64,768]{1,0:T(8,128)(2,1)S(1)}, u32[]{:S(2)}, u32[]{:S(2)}) collective-permute-start(bf16[64,768]{1,0:T(8,128)(2,1)S(1)} %collective-permute-done.4), channel_id=1, source_target_pairs={{0,1},{1,2},{2,3},{3,4},{4,5},{5,6},{6,7},{7,8},{8,9},{9,10},{10,1... | collective-permute-start | bytes 294920 | tf_op jit(solution)/shard_map/ppermute | solution.py:54
  49.6 35.7 %collective-permute-start.6 = (bf16[64,768]{1,0:T(8,128)(2,1)S(1)}, bf16[64,768]{1,0:T(8,128)(2,1)}, u32[]{:S(2)}, u32[]{:S(2)}) collective-permute-start(bf16[64,768]{1,0:T(8,128)(2,1)S(1)} %collective-permute-done.5), channel_id=1, source_target_pairs={{0,1},{1,2},{2,3},{3,4},{4,5},{5,6},{6,7},{7,8},{8,9},{9,10},{10,1... | collective-permute-start | bytes 294920 | tf_op jit(solution)/shard_map/ppermute | solution.py:54
  85.3 17.4 %collective-permute-start.7 = (bf16[64,768]{1,0:T(8,128)(2,1)}, bf16[64,768]{1,0:T(8,128)(2,1)}, u32[]{:S(2)}, u32[]{:S(2)}) collective-permute-start(bf16[64,768]{1,0:T(8,128)(2,1)} %collective-permute-done.6), channel_id=1, source_target_pairs={{0,1},{1,2},{2,3},{3,4},{4,5},{5,6},{6,7},{7,8},{8,9},{9,10},{10,1... | collective-permute-start | bytes 294920 | tf_op jit(solution)/shard_map/ppermute | solution.py:54
  102.7 7.1 %collective-permute-start.8 = (bf16[64,768]{1,0:T(8,128)(2,1)}, bf16[64,768]{1,0:T(8,128)(2,1)}, u32[]{:S(2)}, u32[]{:S(2)}) collective-permute-start(bf16[64,768]{1,0:T(8,128)(2,1)} %collective-permute-done.7), channel_id=1, source_target_pairs={{0,1},{1,2},{2,3},{3,4},{4,5},{5,6},{6,7},{7,8},{8,9},{9,10},{10,1... | collective-permute-start | bytes 294920 | tf_op jit(solution)/shard_map/ppermute | solution.py:54
  109.8 6.9 %collective-permute-start.9 = (bf16[64,768]{1,0:T(8,128)(2,1)}, bf16[64,768]{1,0:T(8,128)(2,1)S(1)}, u32[]{:S(2)}, u32[]{:S(2)}) collective-permute-start(bf16[64,768]{1,0:T(8,128)(2,1)} %collective-permute-done.8), channel_id=1, source_target_pairs={{0,1},{1,2},{2,3},{3,4},{4,5},{5,6},{6,7},{7,8},{8,9},{9,10},{10,1... | collective-permute-start | bytes 294920 | tf_op jit(solution)/shard_map/ppermute | solution.py:54
  116.8 6.7 %collective-permute-start.10 = (bf16[64,768]{1,0:T(8,128)(2,1)S(1)}, bf16[64,768]{1,0:T(8,128)(2,1)S(1)}, u32[]{:S(2)}, u32[]{:S(2)}) collective-permute-start(bf16[64,768]{1,0:T(8,128)(2,1)S(1)} %collective-permute-done.9), channel_id=1, source_target_pairs={{0,1},{1,2},{2,3},{3,4},{4,5},{5,6},{6,7},{7,8},{8,9},{9,10},{10,1... | collective-permute-start | bytes 294920 | tf_op jit(solution)/shard_map/ppermute | solution.py:54
  121.3 222.4 %reduce-scatter.5.cloned.1.call-start = ((), (), s32[]{:S(2)}) async-start(), calls=%async_computation.3 | async-start | bytes 3342336 | tf_op jit(solution)/shard_map/reduce_scatter | solution.py:65
  123.5 6.7 %collective-permute-start.11 = (bf16[64,768]{1,0:T(8,128)(2,1)S(1)}, bf16[64,768]{1,0:T(8,128)(2,1)S(1)}, u32[]{:S(2)}, u32[]{:S(2)}) collective-permute-start(bf16[64,768]{1,0:T(8,128)(2,1)S(1)} %collective-permute-done.10), channel_id=1, source_target_pairs={{0,1},{1,2},{2,3},{3,4},{4,5},{5,6},{6,7},{7,8},{8,9},{9,10},{10,1... | collective-permute-start | bytes 294920 | tf_op jit(solution)/shard_map/ppermute | solution.py:54
  130.3 6.7 %collective-permute-start.12 = (bf16[64,768]{1,0:T(8,128)(2,1)S(1)}, bf16[64,768]{1,0:T(8,128)(2,1)S(1)}, u32[]{:S(2)}, u32[]{:S(2)}) collective-permute-start(bf16[64,768]{1,0:T(8,128)(2,1)S(1)} %collective-permute-done.11), channel_id=1, source_target_pairs={{0,1},{1,2},{2,3},{3,4},{4,5},{5,6},{6,7},{7,8},{8,9},{9,10},{10,1... | collective-permute-start | bytes 294920 | tf_op jit(solution)/shard_map/ppermute | solution.py:54
  137.0 6.7 %collective-permute-start.13 = (bf16[64,768]{1,0:T(8,128)(2,1)S(1)}, bf16[64,768]{1,0:T(8,128)(2,1)S(1)}, u32[]{:S(2)}, u32[]{:S(2)}) collective-permute-start(bf16[64,768]{1,0:T(8,128)(2,1)S(1)} %collective-permute-done.12), channel_id=1, source_target_pairs={{0,1},{1,2},{2,3},{3,4},{4,5},{5,6},{6,7},{7,8},{8,9},{9,10},{10,1... | collective-permute-start | bytes 294920 | tf_op jit(solution)/shard_map/ppermute | solution.py:54
  143.7 6.7 %collective-permute-start.14 = (bf16[64,768]{1,0:T(8,128)(2,1)S(1)}, bf16[64,768]{1,0:T(8,128)(2,1)S(1)}, u32[]{:S(2)}, u32[]{:S(2)}) collective-permute-start(bf16[64,768]{1,0:T(8,128)(2,1)S(1)} %collective-permute-done.13), channel_id=1, source_target_pairs={{0,1},{1,2},{2,3},{3,4},{4,5},{5,6},{6,7},{7,8},{8,9},{9,10},{10,1... | collective-permute-start | bytes 294920 | tf_op jit(solution)/shard_map/ppermute | solution.py:54
  192.1 6.8 %collective-permute-start.15 = (bf16[64,768]{1,0:T(8,128)(2,1)S(1)}, bf16[64,768]{1,0:T(8,128)(2,1)S(1)}, u32[]{:S(2)}, u32[]{:S(2)}) collective-permute-start(bf16[64,768]{1,0:T(8,128)(2,1)S(1)} %fusion.16), channel_id=1, source_target_pairs={{0,1},{1,2},{2,3},{3,4},{4,5},{5,6},{6,7},{7,8},{8,9},{9,10},{10,1... | collective-permute-start | bytes 294920 | tf_op jit(solution)/shard_map/ppermute | solution.py:54
  198.9 6.7 %collective-permute-start.16 = (bf16[64,768]{1,0:T(8,128)(2,1)S(1)}, bf16[64,768]{1,0:T(8,128)(2,1)S(1)}, u32[]{:S(2)}, u32[]{:S(2)}) collective-permute-start(bf16[64,768]{1,0:T(8,128)(2,1)S(1)} %collective-permute-done.15), channel_id=1, source_target_pairs={{0,1},{1,2},{2,3},{3,4},{4,5},{5,6},{6,7},{7,8},{8,9},{9,10},{10,1... | collective-permute-start | bytes 294920 | tf_op jit(solution)/shard_map/ppermute | solution.py:54
  205.7 6.7 %collective-permute-start.17 = (bf16[64,768]{1,0:T(8,128)(2,1)S(1)}, bf16[64,768]{1,0:T(8,128)(2,1)S(1)}, u32[]{:S(2)}, u32[]{:S(2)}) collective-permute-start(bf16[64,768]{1,0:T(8,128)(2,1)S(1)} %collective-permute-done.16), channel_id=1, source_target_pairs={{0,1},{1,2},{2,3},{3,4},{4,5},{5,6},{6,7},{7,8},{8,9},{9,10},{10,1... | collective-permute-start | bytes 294920 | tf_op jit(solution)/shard_map/ppermute | solution.py:54
  212.4 6.7 %collective-permute-start.18 = (bf16[64,768]{1,0:T(8,128)(2,1)S(1)}, bf16[64,768]{1,0:T(8,128)(2,1)S(1)}, u32[]{:S(2)}, u32[]{:S(2)}) collective-permute-start(bf16[64,768]{1,0:T(8,128)(2,1)S(1)} %collective-permute-done.17), channel_id=1, source_target_pairs={{0,1},{1,2},{2,3},{3,4},{4,5},{5,6},{6,7},{7,8},{8,9},{9,10},{10,1... | collective-permute-start | bytes 294920 | tf_op jit(solution)/shard_map/ppermute | solution.py:54
  219.8 6.7 %collective-permute-start.19 = (bf16[64,768]{1,0:T(8,128)(2,1)S(1)}, bf16[64,768]{1,0:T(8,128)(2,1)S(1)}, u32[]{:S(2)}, u32[]{:S(2)}) collective-permute-start(bf16[64,768]{1,0:T(8,128)(2,1)S(1)} %collective-permute-done.18), channel_id=1, source_target_pairs={{0,1},{1,2},{2,3},{3,4},{4,5},{5,6},{6,7},{7,8},{8,9},{9,10},{10,1... | collective-permute-start | bytes 294920 | tf_op jit(solution)/shard_map/ppermute | solution.py:54
  227.2 6.7 %collective-permute-start.20 = (bf16[64,768]{1,0:T(8,128)(2,1)S(1)}, bf16[64,768]{1,0:T(8,128)(2,1)S(1)}, u32[]{:S(2)}, u32[]{:S(2)}) collective-permute-start(bf16[64,768]{1,0:T(8,128)(2,1)S(1)} %collective-permute-done.19), channel_id=1, source_target_pairs={{0,1},{1,2},{2,3},{3,4},{4,5},{5,6},{6,7},{7,8},{8,9},{9,10},{10,1... | collective-permute-start | bytes 294920 | tf_op jit(solution)/shard_map/ppermute | solution.py:54
  234.5 6.7 %collective-permute-start.21 = (bf16[64,768]{1,0:T(8,128)(2,1)S(1)}, bf16[64,768]{1,0:T(8,128)(2,1)S(1)}, u32[]{:S(2)}, u32[]{:S(2)}) collective-permute-start(bf16[64,768]{1,0:T(8,128)(2,1)S(1)} %collective-permute-done.20), channel_id=1, source_target_pairs={{0,1},{1,2},{2,3},{3,4},{4,5},{5,6},{6,7},{7,8},{8,9},{9,10},{10,1... | collective-permute-start | bytes 294920 | tf_op jit(solution)/shard_map/ppermute | solution.py:54
  241.3 6.8 %collective-permute-start.22 = (bf16[64,768]{1,0:T(8,128)(2,1)S(1)}, bf16[64,768]{1,0:T(8,128)(2,1)}, u32[]{:S(2)}, u32[]{:S(2)}) collective-permute-start(bf16[64,768]{1,0:T(8,128)(2,1)S(1)} %collective-permute-done.21), channel_id=1, source_target_pairs={{0,1},{1,2},{2,3},{3,4},{4,5},{5,6},{6,7},{7,8},{8,9},{9,10},{10,1... | collective-permute-start | bytes 294920 | tf_op jit(solution)/shard_map/ppermute | solution.py:54
  248.1 17.4 %collective-permute-start.23 = (bf16[64,768]{1,0:T(8,128)(2,1)}, bf16[64,768]{1,0:T(8,128)(2,1)}, u32[]{:S(2)}, u32[]{:S(2)}) collective-permute-start(bf16[64,768]{1,0:T(8,128)(2,1)} %collective-permute-done.22), channel_id=1, source_target_pairs={{0,1},{1,2},{2,3},{3,4},{4,5},{5,6},{6,7},{7,8},{8,9},{9,10},{10,1... | collective-permute-start | bytes 294920 | tf_op jit(solution)/shard_map/ppermute | solution.py:54
  265.5 7.3 %collective-permute-start.24 = (bf16[64,768]{1,0:T(8,128)(2,1)}, bf16[64,768]{1,0:T(8,128)(2,1)}, u32[]{:S(2)}, u32[]{:S(2)}) collective-permute-start(bf16[64,768]{1,0:T(8,128)(2,1)} %collective-permute-done.23), channel_id=1, source_target_pairs={{0,1},{1,2},{2,3},{3,4},{4,5},{5,6},{6,7},{7,8},{8,9},{9,10},{10,1... | collective-permute-start | bytes 294920 | tf_op jit(solution)/shard_map/ppermute | solution.py:54
  272.8 6.9 %collective-permute-start.25 = (bf16[64,768]{1,0:T(8,128)(2,1)}, bf16[64,768]{1,0:T(8,128)(2,1)S(1)}, u32[]{:S(2)}, u32[]{:S(2)}) collective-permute-start(bf16[64,768]{1,0:T(8,128)(2,1)} %collective-permute-done.24), channel_id=1, source_target_pairs={{0,1},{1,2},{2,3},{3,4},{4,5},{5,6},{6,7},{7,8},{8,9},{9,10},{10,1... | collective-permute-start | bytes 294920 | tf_op jit(solution)/shard_map/ppermute | solution.py:54
  279.8 6.7 %collective-permute-start.26 = (bf16[64,768]{1,0:T(8,128)(2,1)S(1)}, bf16[64,768]{1,0:T(8,128)(2,1)S(1)}, u32[]{:S(2)}, u32[]{:S(2)}) collective-permute-start(bf16[64,768]{1,0:T(8,128)(2,1)S(1)} %collective-permute-done.25), channel_id=1, source_target_pairs={{0,1},{1,2},{2,3},{3,4},{4,5},{5,6},{6,7},{7,8},{8,9},{9,10},{10,1... | collective-permute-start | bytes 294920 | tf_op jit(solution)/shard_map/ppermute | solution.py:54
  286.5 6.7 %collective-permute-start.27 = (bf16[64,768]{1,0:T(8,128)(2,1)S(1)}, bf16[64,768]{1,0:T(8,128)(2,1)S(1)}, u32[]{:S(2)}, u32[]{:S(2)}) collective-permute-start(bf16[64,768]{1,0:T(8,128)(2,1)S(1)} %collective-permute-done.26), channel_id=1, source_target_pairs={{0,1},{1,2},{2,3},{3,4},{4,5},{5,6},{6,7},{7,8},{8,9},{9,10},{10,1... | collective-permute-start | bytes 294920 | tf_op jit(solution)/shard_map/ppermute | solution.py:54
  293.3 6.7 %collective-permute-start.28 = (bf16[64,768]{1,0:T(8,128)(2,1)S(1)}, bf16[64,768]{1,0:T(8,128)(2,1)S(1)}, u32[]{:S(2)}, u32[]{:S(2)}) collective-permute-start(bf16[64,768]{1,0:T(8,128)(2,1)S(1)} %collective-permute-done.27), channel_id=1, source_target_pairs={{0,1},{1,2},{2,3},{3,4},{4,5},{5,6},{6,7},{7,8},{8,9},{9,10},{10,1... | collective-permute-start | bytes 294920 | tf_op jit(solution)/shard_map/ppermute | solution.py:54
  300.0 6.7 %collective-permute-start.29 = (bf16[64,768]{1,0:T(8,128)(2,1)S(1)}, bf16[64,768]{1,0:T(8,128)(2,1)S(1)}, u32[]{:S(2)}, u32[]{:S(2)}) collective-permute-start(bf16[64,768]{1,0:T(8,128)(2,1)S(1)} %collective-permute-done.28), channel_id=1, source_target_pairs={{0,1},{1,2},{2,3},{3,4},{4,5},{5,6},{6,7},{7,8},{8,9},{9,10},{10,1... | collective-permute-start | bytes 294920 | tf_op jit(solution)/shard_map/ppermute | solution.py:54
  (17 other events, 421.1 us)
Sparse Core Ops, SparseCore 0:
  121.4 67.8 reduce-scatter.2
  276.3 67.3 reduce-scatter.4
